TPU v7x, 256 devices: a whole 4x4x8 slice. The times are simulated.
256 devices in a mesh: row: 16 (over z, x_hi), col: 16 (over y, x_lo, core).
Axes of the slice: x: 4 (x_hi: 2, x_lo: 2; x = x_hi * 2 + x_lo), y: 4, z: 8, core: 2. Of those that a mesh axis runs over, the one named last changes fastest.
Arguments:
- front_base: float32 [8, 16, 128, 8, 16, 128], P(None, 'row', None, None, 'col')
- traces: bfloat16 [8, 16, 4, 3, 128, 128], P(None, 'row'), may hold values from -0.75 to 0.75
- adjacency: int32 [128, 4], replicated, may hold values from 0 to 127, as said below
- pivot_order: int32 [2, 512], replicated, may hold values from 0 to 511, each once within a row
- pivot_kind: int32 [2, 512], replicated, may hold values from 0 to 2, as said below
- inverse_diagonal: float32 [2, 512], replicated, may hold values from -0.3 to 0.3
- inverse_coupling: float32 [2, 512], replicated, may hold values from -0.3 to 0.3
- readers: int32 [2, 128], replicated, may hold values 0 or 1
Outputs:
- trailing: float32 [8, 16, 128, 8, 16, 128], P(None, 'row', None, None, 'col')
Inputs may be any that keep to these rules, and one draw needn't show every extreme that they name: The elements form a 16 x 8 grid that closes on itself in both dimensions, numbered in a drawn order; faces 0 and 1 lead to the next and previous element along the first dimension, 2 and 3 along the second, so adjacency[adjacency[e, f], f with its lowest bit flipped] = e. `pivot_kind`: 0 marks a 1 x 1 pivot; 1 marks the first position of a 2 x 2 pivot, whose second position follows and is marked 2; 2 x 2 pivots start at even positions.
All inputs are finite; a program needn't handle non-finite values.
Results may differ from a plain program's by a relative error of at most 0.008.
Values may be sent and summed in bfloat16 or wider, within the bound.
No kernel may reach another device: no remote copies, remote signals or barrier semaphores. Data moves between devices by JAX's collectives and lax.ppermute only.
A program may use at most 128 MiB of HBM per device.

v0:
```python
import jax
import jax.numpy as jnp
from jax import lax
from jax.sharding import PartitionSpec as P

NB = 128
PW = 512
PANELS = 2


def from_root(array, axis, root):
    mine = lax.axis_index(axis) == root
    return lax.psum(jnp.where(mine, array, jnp.zeros_like(array)), axis)


def face_left(values):
    return jnp.concatenate(
        [values[:, :, 0], values[:, :, 0], values[:, :, 1], values[:, :, 2]], axis=2
    )


def face_right(values):
    return jnp.concatenate(
        [
            4.0 * values[:, :, 0],
            -0.5 * values[:, :, 1],
            -0.5 * values[:, :, 0],
            2.0 * values[:, :, 2],
        ],
        axis=2,
    )


def apply_inverse(values, pivot_kinds, diagonal, pair_terms):
    starts = (pivot_kinds == 1).astype(values.dtype)
    upward = pair_terms * starts
    upward_prev = jnp.concatenate([jnp.zeros_like(upward[:1]), upward[:-1]])
    following = jnp.concatenate([values[:, 1:], jnp.zeros_like(values[:, :1])], axis=1)
    preceding = jnp.concatenate([jnp.zeros_like(values[:, :1]), values[:, :-1]], axis=1)
    return values * diagonal + following * upward + preceding * upward_prev


def local(
    front_base,
    traces,
    adjacency,
    pivot_order,
    pivot_kind,
    inverse_diagonal,
    inverse_coupling,
    readers,
):
    row_count = lax.axis_size("row")
    col_count = lax.axis_size("col")
    row_index = lax.axis_index("row")
    col_index = lax.axis_index("col")
    row_blocks = front_base.shape[0]
    col_blocks = front_base.shape[3]
    rows_total = row_blocks * NB
    local_traces = traces[:, 0]
    copy_index = 0
    received = [from_root(local_traces, "row", col_index + copy_index * col_count)]
    column_traces = jnp.stack(received, axis=1).reshape((col_blocks,) + local_traces.shape[1:])
    left_parts = face_left(local_traces)
    right_parts = face_right(local_traces)
    column_right = face_right(column_traces)
    opposite = jnp.array([1, 0, 3, 2], dtype=jnp.int32)
    local_elements = jnp.arange(row_blocks, dtype=jnp.int32) * row_count + row_index
    neighbour = jnp.take(adjacency, local_elements, axis=0)
    held_here = neighbour % col_count == col_index
    col_slot = neighbour // col_count
    partner = column_right[col_slot, opposite[None, :]]
    coupling = jnp.einsum(
        "efqi,efqj->efij", left_parts, partner, preferred_element_type=jnp.float32
    )
    self_terms = jnp.einsum(
        "efqi,efqj->eij", left_parts, right_parts, preferred_element_type=jnp.float32
    )
    slot_ids = jnp.arange(col_blocks, dtype=jnp.int32)
    place_pair = (held_here[:, :, None] & (col_slot[:, :, None] == slot_ids[None, None, :])).astype(
        jnp.float32
    )
    self_here = (local_elements % col_count == col_index)[:, None]
    place_self = (self_here & ((local_elements // col_count)[:, None] == slot_ids[None, :])).astype(
        jnp.float32
    )
    assembled = jnp.einsum("eij,ec->eicj", self_terms, place_self, precision=lax.Precision.HIGHEST)
    assembled = assembled - jnp.einsum(
        "efij,efc->eicj", coupling, place_pair, precision=lax.Precision.HIGHEST
    )
    front_mat = front_base.reshape(rows_total, col_blocks * NB) + assembled.reshape(
        rows_total, col_blocks * NB
    )
    panel_blocks = PW // NB
    for which_panel in range(PANELS):
        first_block = which_panel * panel_blocks
        front_slots = front_mat.reshape(rows_total, col_blocks, NB)
        low_slot = first_block // col_count
        high_slot = (first_block + panel_blocks - 1) // col_count
        slab_cols = front_slots[:, low_slot : high_slot + 1, :].astype(jnp.bfloat16)[:, :, None, :]
        gathered = lax.all_gather(slab_cols, "col", axis=2, tiled=True)
        gathered = gathered.reshape(rows_total, -1, NB)
        begin_block = first_block - low_slot * col_count
        columns = gathered[:, begin_block : begin_block + panel_blocks, :].reshape(rows_total, PW)
        columns = jnp.take(columns, pivot_order[which_panel], axis=1)
        kept_blocks = jnp.take(readers[which_panel], local_elements) * (
            local_elements >= first_block + panel_blocks
        ).astype(jnp.int32)
        kept_rows = jnp.repeat(kept_blocks, NB).astype(jnp.bfloat16)
        panel_vals = columns * kept_rows[:, None]
        scaled = apply_inverse(
            panel_vals.astype(jnp.float32),
            pivot_kind[which_panel],
            inverse_diagonal[which_panel],
            inverse_coupling[which_panel],
        ).astype(jnp.bfloat16)
        copy_index = 0
        incoming = from_root(panel_vals, "row", col_index + copy_index * col_count)
        transposed = [incoming.reshape(row_blocks, NB, PW)]
        col_panel = jnp.stack(transposed, axis=1).reshape(col_blocks * NB, PW)
        front_mat = front_mat - lax.dot_general(
            scaled, col_panel, (((1,), (1,)), ((), ())), preferred_element_type=jnp.float32
        )
    return front_mat.reshape(row_blocks, 1, NB, col_blocks, 1, NB)


def solution(mesh):
    in_specs = (
        P(None, "row", None, None, "col", None),
        P(None, "row", None, None, None, None),
        P(),
        P(),
        P(),
        P(),
        P(),
        P(),
    )
    out_specs = P(None, "row", None, None, "col", None)
    return jax.shard_map(local, mesh=mesh, in_specs=in_specs, out_specs=out_specs, check_vma=False)
```

profile of v0, /device:TPU:8, one launch (start us, length us, event | category | flops | bytes accessed | tf_op | source)
XLA Modules:
  0.0 654.4 jit_solution(11187019615183884576)
XLA Ops:
  6.5 3.8 broadcast_select_fusion
  10.4 2.1 copy.69
  13.5 5.0 copy.39
  20.8 2.8 fusion.10
  23.6 169.1 %all-reduce.8.cloned.1.call-done = bf16[8,4,3,128,128]{4,3,1,0,2:T(8,128)(2,1)} async-done(((bf16[8,4,3,128,128]{4,3,1,0,2:T(8,128)(2,1)}), bf16[8,4,3,128,128]{4,3,1,0,2:T(8,128)(2,1)}) %all-reduce.8.cloned.1.call-update) | async-done | bytes 3145744 | tf_op jit(solution)/shard_map/psum | solution.py:13
  192.7 2.2 multiply_bitcast_fusion.1
  194.9 2.2 pad_maximum_fusion.1
  197.1 5.4 gather_fusion.1
  202.6 3.2 fusion.9
  205.8 4.5 multiply_subtract_fusion
  215.4 36.0 %all-gather.5.cloned.1.call-done = bf16[1024,16,128]{2,0,1:T(8,128)(2,1)} async-done(((bf16[1024,1,128]{2,0,1:T(8,128)(2,1)}), bf16[1024,16,128]{2,0,1:T(8,128)(2,1)}) %all-gather.5.cloned.1.call-update) | async-done | bytes 4194320 | tf_op jit(solution)/shard_map/all_gather | solution.py:101
  256.8 5.2 copy.68
  262.0 5.4 copy.51
  267.5 5.3 copy.67
  272.8 5.5 copy.38
  278.2 2.4 fusion.50
  280.6 137.7 %all-reduce.10.cloned.1.call-done = bf16[1024,512]{0,1:T(8,128)(2,1)} async-done(((bf16[1024,512]{0,1:T(8,128)(2,1)}), bf16[1024,512]{0,1:T(8,128)(2,1)}) %all-reduce.10.cloned.1.call-update) | async-done | bytes 1048592 | tf_op jit(solution)/shard_map/psum | solution.py:13
  418.4 8.7 %fusion.53 = (bf16[1024,1024]{0,1:T(8,128)(2,1)S(1)}, f32[1024,1024]{0,1:T(8,128)}) fusion(bf16[1024,512]{0,1:T(8,128)(2,1)} %all-reduce.10.cloned.1.call-done, f32[1024,511]{0,1:T(8,128)} %get-tuple-element.21, f32[1024,511]{0,1:T(8,128)} %get-tuple-element.20, f32[512]{0:T(512)S(1)} %pad_maximum_fusion.7, f32[512]{0:T(512)S(1)} %bitcast.126, ...), kind=kOutput, calls=%fused_computation.126 | convolution fusion | flops 1081606144 | bytes 20972032 | tf_op jit(solution)/shard_map/dot_general | solution.py:121
  428.8 36.9 %all-gather.7.cloned.1.call-done = bf16[1024,16,128]{2,0,1:T(8,128)(2,1)} async-done(((bf16[1024,1,128]{2,0,1:T(8,128)(2,1)}), bf16[1024,16,128]{2,0,1:T(8,128)(2,1)}) %all-gather.7.cloned.1.call-update) | async-done | bytes 4194320 | tf_op jit(solution)/shard_map/all_gather | solution.py:101
  471.0 2.3 fusion.49
  473.3 159.0 %all-reduce.12.cloned.1.call-done = bf16[1024,512]{0,1:T(8,128)(2,1)} async-done(((bf16[1024,512]{0,1:T(8,128)(2,1)}), bf16[1024,512]{0,1:T(8,128)(2,1)}) %all-reduce.12.cloned.1.call-update) | async-done | bytes 1048592 | tf_op jit(solution)/shard_map/psum | solution.py:13
  632.3 5.5 subtract_bitcast_fusion
  637.7 3.0 copy.56
  640.7 7.2 %copy.45 = f32[8,1,128,8,1,128]{5,4,3,2,1,0:T(1,128)} copy(f32[8,1,128,8,1,128]{2,0,5,3,4,1:T(8,128)} %bitcast.118) | data formatting | bytes 8388608 | tf_op jit(solution)/shard_map/reshape | solution.py:124
  (86 shorter events, 20.7 us)
Async XLA Ops:
  6.5 186.2 %all-reduce.8.cloned.1.call-start = ((), (), s32[]{:S(2)}) async-start(), calls=%async_computation | async-start | bytes 6291456 | tf_op jit(solution)/shard_map/psum | solution.py:13
  10.3 2.2 copy-start.12
  10.3 3.0 copy-start.14
  10.3 241.0 %all-gather.5.cloned.1.call-start = ((), (), s32[]{:S(2)}) async-start(), calls=%async_computation.3 | async-start | bytes 4456448 | tf_op jit(solution)/shard_map/all_gather | solution.py:101
  19.1 1.0 copy-start.1
  19.2 1.3 copy-start.3
  19.2 1.7 copy-start.5
  197.1 5.4 copy-start.2
  197.1 5.4 copy-start.4
  197.1 5.4 copy-start.6
  202.6 3.2 copy-start.7
  205.8 8.8 %copy-start.13 = (s32[2,128]{1,0:T(2,128)S(1)}, s32[2,128]{1,0:T(2,128)}, u32[]{:S(2)}) copy-start(s32[2,128]{1,0:T(2,128)} %param.20) | copy-start | bytes 3076
  205.8 9.4 %copy-start.10 = (s32[2,512]{1,0:T(2,128)S(1)}, s32[2,512]{1,0:T(2,128)}, u32[]{:S(2)}) copy-start(s32[2,512]{1,0:T(2,128)} %param.16) | copy-start | bytes 12292
  210.4 2.0 copy-start
  214.5 203.9 %all-reduce.10.cloned.1.call-start = ((), (), s32[]{:S(2)}) async-start(), calls=%async_computation.1 | async-start | bytes 2097152 | tf_op jit(solution)/shard_map/psum | solution.py:13
  256.6 209.1 %all-gather.7.cloned.1.call-start = ((), (), s32[]{:S(2)}) async-start(), calls=%async_computation.4 | async-start | bytes 4456448 | tf_op jit(solution)/shard_map/all_gather | solution.py:101
  262.0 5.4 copy-start.8
  262.0 5.4 copy-start.9
  262.0 5.5 copy-start.11
  428.0 204.3 %all-reduce.12.cloned.1.call-start = ((), (), s32[]{:S(2)}) async-start(), calls=%async_computation.2 | async-start | bytes 2097152 | tf_op jit(solution)/shard_map/psum | solution.py:13
Sparse Core Ops, SparseCore 0:
  10.4 182.2 all-reduce.7
  214.6 36.6 all-gather.4
  256.7 161.6 all-reduce.9
  428.1 37.5 all-gather.6
  471.0 161.2 all-reduce.11
where the time goes:
time: 655 us; the launch traced here: 654 us
  waiting for transfers between devices  539 us (82%)
  local copies, waits for them, and re-layouts  63.8 us (10%)
  matrix products  24.7 us (4%)
  other arithmetic  13.4 us (2%)
  between operations  13.4 us (2%)
    psum x3, waiting for transfers between devices, from_root(): return lax.psum(jnp.where(mine, array, jnp.zeros_like(array)), axis)  466 us
    all_gather x2, waiting for transfers between devices, local(): gathered = lax.all_gather(slab_cols, 'col', axis=2, tiled=True)  72.9 us
    unnamed x37, local copies, waits for them, and re-layouts  24.8 us
    dot_general x2, matrix products, local(): lax.dot_general(scaled, col_panel, (((1,), (1,)), ((), ())), preferred_el...  14.2 us
  transfers between devices with their start and end apart: 5, of which 5 were waited for; matrix products, arithmetic and copies ran while one was open for 6% of the time, Pallas kernels for 0%

commit v1 on v0

--- a/solution.py
+++ b/solution.py
@@ -10,7 +10,7 @@
 
 def from_root(array, axis, root):
     mine = lax.axis_index(axis) == root
-    return lax.psum(jnp.where(mine, array, jnp.zeros_like(array)), axis)
+    return jnp.sum(lax.all_gather(jnp.where(mine, array, jnp.zeros_like(array)), axis), axis=0)
 
 
 def face_left(values):

time: 655 us -> 1260 us (1.92)
  waiting for transfers between devices: 539 us -> 1090 us
  local copies, waits for them, and re-layouts: 63.8 us -> 95.2 us
  other arithmetic: 13.4 us -> 42.7 us
    all_gather x0 -> x3, waiting for transfers between devices: none -> 1020 us  [from_root(): lax.all_gather(jnp.where(mine, array, jnp.zeros_like(array)), axis)]
    psum x3 -> x0, waiting for transfers between devices: 466 us -> none  [from_root(): return lax.psum(jnp.where(mine, array, jnp.zeros_like(array)), axis)]
    reduce_sum x0 -> x3, other arithmetic: none -> 33.1 us  [from_root(): jnp.sum(lax.all_gather(jnp.where(mine, array, jnp.zeros_like(array)), axi...]
    unnamed x37 -> x53, local copies, waits for them, and re-layouts: 24.8 us -> 56.4 us
  transfers between devices with their start and end apart: 5 -> 5, of which waited for: 5 -> 5; matrix products, arithmetic and copies ran while one was open for 6% -> 3% of each run, Pallas kernels for 0% -> 0%
where the time goes in v1:
time: 1260 us; the launch traced here: 1250 us
  waiting for transfers between devices  1090 us (87%)
  local copies, waits for them, and re-layouts  95.2 us (8%)
  other arithmetic  42.7 us (3%)
  matrix products  16.3 us (1%)
  between operations  13.6 us (1%)
    all_gather x3, waiting for transfers between devices, from_root(): lax.all_gather(jnp.where(mine, array, jnp.zeros_like(array)), axis)  1020 us
    all_gather x2, waiting for transfers between devices, local(): gathered = lax.all_gather(slab_cols, 'col', axis=2, tiled=True)  70.8 us
    unnamed x53, local copies, waits for them, and re-layouts  56.4 us
    reduce_sum x3, other arithmetic, from_root(): jnp.sum(lax.all_gather(jnp.where(mine, array, jnp.zeros_like(array)), axi...  33.1 us
  transfers between devices with their start and end apart: 5, of which 5 were waited for; matrix products, arithmetic and copies ran while one was open for 3% of the time, Pallas kernels for 0%

profile of v1, /device:TPU:8, one launch (start us, length us, event | category | flops | bytes accessed | tf_op | source)
XLA Modules:
  0.0 1254.5 jit_solution(8074282746524687926)
XLA Ops:
  11.7 5.1 copy.45
  19.0 2.8 fusion.10
  21.7 591.6 %all-gather.11.cloned.1.call-done = bf16[128,1,4,3,128,128]{5,4,3,2,1,0:T(8,128)(2,1)} async-done(((bf16[8,1,4,3,128,128]{5,4,3,2,1,0:T(8,128)(2,1)}), bf16[128,1,4,3,128,128]{5,4,3,2,1,0:T(8,128)(2,1)}) %all-gather.11.cloned.1.call-update) | async-done | bytes 50331664 | tf_op jit(solution)/shard_map/all_gather | solution.py:13
  613.4 16.8 %bitcast_reduce_fusion = bf16[8,4,3,128,128]{4,3,2,1,0:T(8,128)(2,1)S(1)} fusion(bf16[16,8,4,3,128,128]{5,4,3,2,1,0:T(8,128)(2,1)} %bitcast.135), kind=kLoop, calls=%fused_computation.6 | loop fusion | flops 23592960 | bytes 53477376 | tf_op jit(solution)/shard_map/reduce_sum | solution.py:13
  632.8 5.4 gather_fusion.1
  638.2 3.2 fusion.9
  641.4 4.5 multiply_subtract_fusion
  651.2 35.4 %all-gather.13.cloned.1.call-done = bf16[1024,16,128]{2,0,1:T(8,128)(2,1)} async-done(((bf16[1024,1,128]{2,0,1:T(8,128)(2,1)}), bf16[1024,16,128]{2,0,1:T(8,128)(2,1)}) %all-gather.13.cloned.1.call-update) | async-done | bytes 4194320 | tf_op jit(solution)/shard_map/all_gather | solution.py:101
  691.8 5.2 copy.76
  697.0 5.5 copy.57
  702.6 5.5 copy.75
  708.0 5.4 copy.44
  713.4 2.4 fusion.51
  715.8 201.0 %all-gather.15.cloned.1.call-done = bf16[16384,512]{0,1:T(8,128)(2,1)} async-done(((bf16[1024,512]{0,1:T(8,128)(2,1)}), bf16[16384,512]{0,1:T(8,128)(2,1)}) %all-gather.15.cloned.1.call-update) | async-done | bytes 16777232 | tf_op jit(solution)/shard_map/all_gather | solution.py:13
  916.7 15.6 %copy.64 = bf16[64,8,16,1024]{3,2,1,0:T(8,128)(2,1)S(1)} copy(bf16[64,8,16,1024]{3,1,2,0:T(8,128)(2,1)} %bitcast.140) | data formatting | bytes 33554432
  932.4 8.1 bitcast_reduce_fusion.2
  940.6 3.9 fusion.54
  946.5 35.4 %all-gather.17.cloned.1.call-done = bf16[1024,16,128]{2,0,1:T(8,128)(2,1)} async-done(((bf16[1024,1,128]{2,0,1:T(8,128)(2,1)}), bf16[1024,16,128]{2,0,1:T(8,128)(2,1)}) %all-gather.17.cloned.1.call-update) | async-done | bytes 4194320 | tf_op jit(solution)/shard_map/all_gather | solution.py:101
  987.1 2.4 fusion.50
  989.5 222.6 %all-gather.19.cloned.1.call-done = bf16[16384,512]{0,1:T(8,128)(2,1)} async-done(((bf16[1024,512]{0,1:T(8,128)(2,1)}), bf16[16384,512]{0,1:T(8,128)(2,1)}) %all-gather.19.cloned.1.call-update) | async-done | bytes 16777232 | tf_op jit(solution)/shard_map/all_gather | solution.py:13
  1212.1 15.6 %copy.65 = bf16[64,8,16,1024]{3,2,1,0:T(8,128)(2,1)S(1)} copy(bf16[64,8,16,1024]{3,1,2,0:T(8,128)(2,1)} %bitcast.141) | data formatting | bytes 33554432
  1227.7 8.1 bitcast_reduce_fusion.1
  1237.8 3.0 copy.66
  1240.8 7.2 copy.51
  (105 shorter events, 29.2 us)
Async XLA Ops:
  6.5 606.8 %all-gather.11.cloned.1.call-start = ((), (), s32[]{:S(2)}) async-start(), calls=%async_computation | async-start | bytes 53477376 | tf_op jit(solution)/shard_map/all_gather | solution.py:13
  8.4 2.2 copy-start.19
  8.4 3.0 copy-start.21
  8.4 678.1 %all-gather.13.cloned.1.call-start = ((), (), s32[]{:S(2)}) async-start(), calls=%async_computation.1 | async-start | bytes 4456448 | tf_op jit(solution)/shard_map/all_gather | solution.py:101
  632.8 5.4 copy-start.9
  632.8 5.4 copy-start.11
  632.8 5.4 copy-start.13
  638.2 3.2 copy-start.14
  641.4 8.9 copy-start.20
  641.4 9.6 copy-start.17
  646.0 2.0 copy-start
  650.1 266.6 %all-gather.15.cloned.1.call-start = ((), (), s32[]{:S(2)}) async-start(), calls=%async_computation.2 | async-start | bytes 17825792 | tf_op jit(solution)/shard_map/all_gather | solution.py:13
  691.7 290.2 %all-gather.17.cloned.1.call-start = ((), (), s32[]{:S(2)}) async-start(), calls=%async_computation.3 | async-start | bytes 4456448 | tf_op jit(solution)/shard_map/all_gather | solution.py:101
  697.0 5.5 copy-start.15
  697.0 5.5 copy-start.16
  697.0 5.6 copy-start.18
  932.4 8.2 copy-start.1
  932.4 8.2 copy-start.2
  932.4 8.2 copy-start.6
  932.4 8.2 copy-start.7
  945.4 266.7 %all-gather.19.cloned.1.call-start = ((), (), s32[]{:S(2)}) async-start(), calls=%async_computation.4 | async-start | bytes 17825792 | tf_op jit(solution)/shard_map/all_gather | solution.py:13
  1227.7 8.2 copy-start.3
  1227.7 8.2 copy-start.4
  1227.7 8.2 copy-start.5
  (3 other events, 3.9 us)
Sparse Core Ops, SparseCore 0:
  9.9 603.3 all-gather.10
  650.2 36.2 all-gather.12
  691.8 224.8 all-gather.14
  945.5 36.2 all-gather.16
  987.2 224.8 all-gather.18

commit v2 on v0

--- a/solution.py
+++ b/solution.py
@@ -98,7 +98,9 @@
         low_slot = first_block // col_count
         high_slot = (first_block + panel_blocks - 1) // col_count
         slab_cols = front_slots[:, low_slot : high_slot + 1, :].astype(jnp.bfloat16)[:, :, None, :]
-        gathered = lax.all_gather(slab_cols, "col", axis=2, tiled=True)
+        gathered = jnp.concatenate(
+            lax.all_to_all(jnp.stack([slab_cols] * lax.axis_size("col")), "col", 0, 0), axis=2
+        )
         gathered = gathered.reshape(rows_total, -1, NB)
         begin_block = first_block - low_slot * col_count
         columns = gathered[:, begin_block : begin_block + panel_blocks, :].reshape(rows_total, PW)

time: 655 us -> 686 us (1.047)
  waiting for transfers between devices: 539 us -> 556 us
  starting transfers between devices: 0.35 us -> 11.8 us
    all_to_all x0 -> x2, waiting for transfers between devices: none -> 95.7 us  [local(): lax.all_to_all(jnp.stack([slab_cols] * lax.axis_size('col')), 'col', 0, 0)]
    all_gather x2 -> x0, waiting for transfers between devices: 72.9 us -> none  [local(): gathered = lax.all_gather(slab_cols, 'col', axis=2, tiled=True)]
    all_to_all x0 -> x2, starting transfers between devices: none -> 11.5 us  [local(): lax.all_to_all(jnp.stack([slab_cols] * lax.axis_size('col')), 'col', 0, 0)]
    unnamed x37 -> x36, local copies, waits for them, and re-layouts: 24.8 us -> 23.9 us
where the time goes in v2:
time: 686 us
  waiting for transfers between devices  556 us (81%)
  local copies, waits for them, and re-layouts  67 us (10%)
  matrix products  24.7 us (4%)
  between operations  13.4 us (2%)
  other arithmetic  12.8 us (2%)
  starting transfers between devices  11.8 us (2%)
    psum x3, waiting for transfers between devices, from_root(): return lax.psum(jnp.where(mine, array, jnp.zeros_like(array)), axis)  460 us
    all_to_all x2, waiting for transfers between devices, local(): lax.all_to_all(jnp.stack([slab_cols] * lax.axis_size('col')), 'col', 0, 0)  95.7 us
    unnamed x36, local copies, waits for them, and re-layouts  23.9 us
    dot_general x2, matrix products, local(): lax.dot_general(scaled, col_panel, (((1,), (1,)), ((), ())), preferred_el...  14.2 us
  transfers between devices with their start and end apart: 5, of which 5 were waited for; matrix products, arithmetic and copies ran while one was open for 6% of the time, Pallas kernels for 0%

profile of v2, /device:TPU:8, one launch (start us, length us, event | category | flops | bytes accessed | tf_op | source)
XLA Modules:
  0.0 685.6 jit_solution(3744273869198161678)
XLA Ops:
  6.5 3.8 broadcast_select_fusion
  13.5 5.0 copy.41
  20.8 2.8 fusion.10
  23.5 169.3 %all-reduce.8.cloned.1.call-done = bf16[8,4,3,128,128]{4,3,1,0,2:T(8,128)(2,1)} async-done(((bf16[8,4,3,128,128]{4,3,1,0,2:T(8,128)(2,1)}), bf16[8,4,3,128,128]{4,3,1,0,2:T(8,128)(2,1)}) %all-reduce.8.cloned.1.call-update) | async-done | bytes 3145744 | tf_op jit(solution)/shard_map/psum | solution.py:13
  197.2 5.4 gather_fusion.1
  202.7 3.2 fusion.9
  205.9 4.5 multiply_subtract_fusion
  214.1 2.5 stack.6
  216.6 6.1 all-to-all-start
  223.8 47.7 %all-to-all-done = bf16[16,1024,1,1,128]{1,4,3,2,0:T(8,128)(2,1)} async-done(((bf16[16,1024,1,1,128]{1,4,3,2,0:T(8,128)(2,1)}), bf16[16,1024,1,1,128]{1,4,3,2,0:T(8,128)(2,1)}, u32[]{:S(2)}, u32[]{:S(2)}) %all-to-all-start) | async-done | bytes 4194336 | tf_op jit(solution)/shard_map/all_to_all | solution.py:102
  276.2 5.2 copy.69
  281.4 5.4 copy.51
  286.9 5.2 copy.68
  292.1 5.5 copy.40
  297.6 2.4 fusion.51
  300.0 134.3 %all-reduce.10.cloned.1.call-done = bf16[1024,512]{0,1:T(8,128)(2,1)} async-done(((bf16[1024,512]{0,1:T(8,128)(2,1)}), bf16[1024,512]{0,1:T(8,128)(2,1)}) %all-reduce.10.cloned.1.call-update) | async-done | bytes 1048592 | tf_op jit(solution)/shard_map/psum | solution.py:13
  434.2 8.7 %fusion.54 = (bf16[1024,1024]{0,1:T(8,128)(2,1)S(1)}, f32[1024,1024]{0,1:T(8,128)}) fusion(bf16[1024,512]{0,1:T(8,128)(2,1)} %all-reduce.10.cloned.1.call-done, f32[1024,511]{0,1:T(8,128)} %get-tuple-element.21, f32[1024,511]{0,1:T(8,128)} %get-tuple-element.20, f32[512]{0:T(512)S(1)} %pad_maximum_fusion.7, f32[512]{0:T(512)S(1)} %bitcast.136, ...), kind=kOutput, calls=%fused_computation.128 | convolution fusion | flops 1081606144 | bytes 20972032 | tf_op jit(solution)/shard_map/dot_general | solution.py:123
  443.0 2.6 stack.7
  445.6 5.4 all-to-all-start.1
  451.8 48.0 %all-to-all-done.1 = bf16[16,1024,1,1,128]{1,4,3,2,0:T(8,128)(2,1)} async-done(((bf16[16,1024,1,1,128]{1,4,3,2,0:T(8,128)(2,1)}), bf16[16,1024,1,1,128]{1,4,3,2,0:T(8,128)(2,1)}, u32[]{:S(2)}, u32[]{:S(2)}) %all-to-all-start.1) | async-done | bytes 4194336 | tf_op jit(solution)/shard_map/all_to_all | solution.py:102
  506.8 156.6 %all-reduce.12.cloned.1.call-done = bf16[1024,512]{0,1:T(8,128)(2,1)} async-done(((bf16[1024,512]{0,1:T(8,128)(2,1)}), bf16[1024,512]{0,1:T(8,128)(2,1)}) %all-reduce.12.cloned.1.call-update) | async-done | bytes 1048592 | tf_op jit(solution)/shard_map/psum | solution.py:13
  663.5 5.5 subtract_bitcast_fusion
  668.9 3.0 copy.55
  671.9 7.2 %copy.45 = f32[8,1,128,8,1,128]{5,4,3,2,1,0:T(1,128)} copy(f32[8,1,128,8,1,128]{2,0,5,3,4,1:T(8,128)} %bitcast.128) | data formatting | bytes 8388608 | tf_op jit(solution)/shard_map/reshape | solution.py:126
  (84 shorter events, 27.0 us)
Async XLA Ops:
  6.5 186.3 %all-reduce.8.cloned.1.call-start = ((), (), s32[]{:S(2)}) async-start(), calls=%async_computation.2 | async-start | bytes 6291456 | tf_op jit(solution)/shard_map/psum | solution.py:13
  10.3 2.2 copy-start.12
  10.3 2.9 copy-start.14
  19.1 1.0 copy-start.1
  19.1 1.3 copy-start.3
  19.1 1.7 copy-start.5
  197.2 5.5 copy-start.2
  197.2 5.5 copy-start.4
  197.2 5.5 copy-start.6
  202.7 3.2 copy-start.7
  210.5 2.0 copy-start
  216.6 6.4 copy-start.13
  216.6 7.0 %copy-start.10 = (s32[2,512]{1,0:T(2,128)S(1)}, s32[2,512]{1,0:T(2,128)}, u32[]{:S(2)}) copy-start(s32[2,512]{1,0:T(2,128)} %param.16) | copy-start | bytes 12292
  216.6 54.9 %all-to-all-start = ((bf16[16,1024,1,1,128]{1,4,3,2,0:T(8,128)(2,1)}), bf16[16,1024,1,1,128]{1,4,3,2,0:T(8,128)(2,1)}, u32[]{:S(2)}, u32[]{:S(2)}) async-start(bf16[16,1024,1,1,128]{1,4,3,2,0:T(8,128)(2,1)} %stack.6), calls=%async_computation | async-start | bytes 8388608 | tf_op jit(solution)/shard_map/all_to_all | solution.py:102
  222.7 211.5 %all-reduce.10.cloned.1.call-start = ((), (), s32[]{:S(2)}) async-start(), calls=%async_computation.3 | async-start | bytes 2097152 | tf_op jit(solution)/shard_map/psum | solution.py:13
  281.4 5.4 copy-start.8
  281.4 5.4 copy-start.9
  281.4 5.5 copy-start.11
  445.6 54.2 %all-to-all-start.1 = ((bf16[16,1024,1,1,128]{1,4,3,2,0:T(8,128)(2,1)}), bf16[16,1024,1,1,128]{1,4,3,2,0:T(8,128)(2,1)}, u32[]{:S(2)}, u32[]{:S(2)}) async-start(bf16[16,1024,1,1,128]{1,4,3,2,0:T(8,128)(2,1)} %stack.7), calls=%async_computation.1 | async-start | bytes 8388608 | tf_op jit(solution)/shard_map/all_to_all | solution.py:102
  451.0 212.5 %all-reduce.12.cloned.1.call-start = ((), (), s32[]{:S(2)}) async-start(), calls=%async_computation.4 | async-start | bytes 2097152 | tf_op jit(solution)/shard_map/psum | solution.py:13
Sparse Core Ops, SparseCore 0:
  10.4 182.3 all-reduce.7
  276.3 157.9 all-reduce.9
  504.5 158.8 all-reduce.11
